TPU v7x, 32 devices: a whole 2x2x4 slice. The times are simulated.
32 devices in a mesh: node: 8 (over z, x), feat: 4 (over y, core).
Axes of the slice: x: 2, y: 2, z: 4, core: 2. Of those that a mesh axis runs over, the one named last changes fastest.
Arguments:
- feature_table: bfloat16 [8192, 2048], P('node', 'feat'), may hold values from -6 to 6
- hub_table: bfloat16 [32, 2048], P('node', 'feat'), may hold values from -6 to 6
- first_self: bfloat16 [2048, 2048], P('feat'), may hold values from -0.125 to 0.125
- first_pooled: bfloat16 [2048, 2048], P('feat'), may hold values from -0.125 to 0.125
- second_self: bfloat16 [2048, 256], P('feat'), may hold values from -0.125 to 0.125
- second_pooled: bfloat16 [2048, 256], P('feat'), may hold values from -0.125 to 0.125
- first_lists: int32 [3072, 10], P('node'), may hold values from 0 to 8223, as said below
- first_counts: int32 [3072], P('node'), may hold values from 1 to 10
- second_lists: int32 [2048, 5], P('node'), may hold values from 0 to 3071, as said below
- second_counts: int32 [2048], P('node'), may hold values from 1 to 5
Outputs:
- embedding: bfloat16 [2048, 256], P(('node', 'feat'))
Inputs may be any that keep to these rules, and one draw needn't show every extreme that they name: `first_lists`: an entry below 8192 names a row of feature_table, held by node shard (entry // 1024); an entry v of 8192 or more names hub clip v - 8192, owned by node shard (v - 8192) // 4. Slots at or beyond a clip's count are padding and still hold such entries. Of the 3840 entries of one node shard's rows, padding included, at most 480 name feature rows held by any one node shard; in every draw one node shard is named exactly 480 times by the rows of every node shard. `second_lists`: entries name frontier clips, held by node shard (entry // 384). Of the 1280 entries of one node shard's rows, padding included, exactly 160 name frontier clips of each node shard.
All inputs are finite; a program needn't handle non-finite values.
Results may differ from a plain program's by a relative error of at most 0.0052.
Values may be sent and summed in bfloat16 or wider, within the bound.
A program may use at most 64 MiB of HBM per device.

v0:
```python
import jax
import jax.numpy as jnp
from jax import lax
from jax.sharding import PartitionSpec as P


def count_matrix(local, width):
    columns = jnp.arange(width, dtype=jnp.int32)[None, :]
    total = jnp.zeros((local.shape[0], width), jnp.float32)
    for k in range(local.shape[1]):
        total = total + (local[:, k : k + 1] == columns).astype(jnp.float32)
    return total.astype(jnp.bfloat16)


def body(
    feature_table,
    hub_table,
    first_self,
    first_pooled,
    second_self,
    second_pooled,
    first_lists,
    first_counts,
    second_lists,
    second_counts,
):
    shards = lax.axis_size("node")
    me = lax.axis_index("node")
    rows_here = feature_table.shape[0]
    hubs_here = hub_table.shape[0]
    front_here, fan_one = first_lists.shape
    targets_here, fan_two = second_lists.shape
    total_rows = rows_here * shards
    slots_one = jnp.arange(fan_one, dtype=jnp.int32)[None, :]
    slots_two = jnp.arange(fan_two, dtype=jnp.int32)[None, :]
    lists_one = jnp.where(slots_one < first_counts[:, None], first_lists, -1)
    lists_two = jnp.where(slots_two < second_counts[:, None], second_lists, -1)
    packed = jnp.concatenate([lists_one.reshape(-1), lists_two.reshape(-1), second_counts]).reshape(
        1, -1
    )
    everyone = lax.all_gather(packed, "node", axis=0, tiled=True)
    cut_one = front_here * fan_one
    cut_two = cut_one + targets_here * fan_two
    all_one = everyone[:, :cut_one].reshape(shards * front_here, fan_one)
    all_two = everyone[:, cut_one:cut_two].reshape(shards * targets_here, fan_two)
    all_counts = everyone[:, cut_two:].reshape(shards * targets_here, 1)
    feature_at = all_one - me * rows_here
    hub_at = all_one - total_rows - me * hubs_here
    local_one = jnp.where(
        (feature_at >= 0) & (feature_at < rows_here) & (all_one >= 0),
        feature_at,
        jnp.where((hub_at >= 0) & (hub_at < hubs_here), hub_at + rows_here, -1),
    )
    combined = jnp.concatenate([feature_table, hub_table], axis=0)
    matrix_one = count_matrix(local_one, rows_here + hubs_here)
    sums = jnp.dot(matrix_one, combined, preferred_element_type=jnp.float32)
    sums = lax.psum_scatter(sums.astype(jnp.bfloat16), "node", scatter_dimension=0, tiled=True)
    first_mean = (sums.astype(jnp.float32) / first_counts[:, None].astype(jnp.float32)).astype(
        jnp.bfloat16
    )
    part = jnp.dot(feature_table[:front_here], first_self, preferred_element_type=jnp.float32)
    part = part + jnp.dot(first_mean, first_pooled, preferred_element_type=jnp.float32)
    hidden = jax.nn.relu(
        lax.psum_scatter(part.astype(jnp.bfloat16), "feat", scatter_dimension=1, tiled=True)
    )
    projected = jnp.dot(hidden, second_pooled, preferred_element_type=jnp.float32)
    own = jnp.dot(hidden[:targets_here], second_self, preferred_element_type=jnp.float32)
    local_two = jnp.where(all_two >= 0, all_two - me * front_here, -1)
    matrix_two = count_matrix(local_two, front_here)
    mixed = jnp.dot(
        matrix_two, projected.astype(jnp.bfloat16), preferred_element_type=jnp.float32
    ) / all_counts.astype(jnp.float32)
    here = lax.dynamic_slice_in_dim(mixed, me * targets_here, targets_here, 0)
    mixed = lax.dynamic_update_slice_in_dim(mixed, here + own, me * targets_here, 0)
    mixed = lax.psum_scatter(mixed, ("node", "feat"), scatter_dimension=0, tiled=True)
    scale = lax.rsqrt(jnp.mean(mixed * mixed, axis=1, keepdims=True) + 1e-06)
    return (mixed * scale).astype(jnp.bfloat16)


def solution(mesh):
    return jax.shard_map(
        body,
        mesh=mesh,
        in_specs=(
            P("node", "feat"),
            P("node", "feat"),
            P("feat", None),
            P("feat", None),
            P("feat", None),
            P("feat", None),
            P("node", None),
            P("node"),
            P("node", None),
            P("node"),
        ),
        out_specs=P(("node", "feat"), None),
        check_vma=False,
    )
```

profile of v0, /device:TPU:0, one launch (start us, length us, event | category | flops | bytes accessed | tf_op | source)
XLA Modules:
  0.0 341.4 jit_solution(16329909199386390386)
XLA Ops:
  6.5 0.9 fusion.27
  7.4 0.1 copy.16
  7.5 0.2 reshape.54
  7.7 0.7 fusion.25
  8.5 0.1 copy.15
  8.6 0.1 reshape.53
  8.8 0.7 pad_add_fusion
  9.5 32.4 %all-gather.1 = s32[8,1,5376]{2,1,0:T(1,128)S(1)} all-gather(s32[1,1,5376]{2,1,0:T(1,128)S(1)} %reshape.59), channel_id=2, replica_groups=mesh['node'=8,'feat'=4] {'node'}, dimensions={0}, use_global_device_ids=true | all-gather | bytes 193536 | tf_op jit(solution)/shard_map/all_gather | solution.py:41
  42.0 1.8 ge.24
  43.8 2.8 reshape.57
  46.6 2.8 sub.31
  49.4 2.3 and_select_fusion
  51.7 7.9 %slice_reduce_fusion.9 = (s32[3072]{0:T(1024)S(1)}, s32[3072]{0:T(1024)S(1)}, s32[3072]{0:T(1024)S(1)}, s32[3072]{0:T(1024)S(1)}, s32[3072]{0:T(1024)S(1)}, /*in...) fusion(s32[3072,10]{1,0:T(8,128)S(1)} %and_select_fusion), kind=kLoop, calls=%fused_computation.40 | loop fusion | bytes 245760 | tf_op jit(solution)/shard_map/slice | solution.py:11
  59.7 19.4 %fusion.11 = bf16[3072,512]{1,0:T(8,128)(2,1)} fusion(s32[3072]{0:T(1024)S(1)} %get-tuple-element.6, s32[3072]{0:T(1024)S(1)} %get-tuple-element.7, s32[3072]{0:T(1024)S(1)} %get-tuple-element.8, s32[3072]{0:T(1024)S(1)} %get-tuple-element.9, s32[3072]{0:T(1024)S(1)} %get-tuple-element.10, s32[3072]{0:T(1024)S(1)} %get-tuple-element.11, ...), kind=kOutput, calls=%fused_computation.22 | convolution fusion | flops 3332227072 | bytes 4321280 | tf_op jit(solution)/shard_map/dot_general | solution.py:56
  79.1 0.0 reduce-scatter.4.cloned.1.call-update
  79.1 0.0 reduce-scatter.6.cloned.1.call-start
  79.1 0.6 copy-done.3
  79.8 3.6 %fusion.22 = f32[384,2048]{1,0:T(8,128)} fusion(bf16[512,2048]{1,0:T(8,128)(2,1)S(1)} %copy-done, bf16[1024,512]{1,0:T(8,128)(2,1)} %param.10), kind=kOutput, calls=%fused_computation.60 | convolution fusion | flops 805306368 | bytes 5636096 | tf_op jit(solution)/shard_map/dot_general | solution.py:61
  83.4 71.1 %reduce-scatter.4.cloned.1.call-done = bf16[384,512]{1,0:T(8,128)(2,1)} async-done(((bf16[3072,512]{1,0:T(8,128)(2,1)}), bf16[384,512]{1,0:T(8,128)(2,1)}) %reduce-scatter.4.cloned.1.call-update) | async-done | bytes 393232 | tf_op jit(solution)/shard_map/reduce_scatter | solution.py:57
  154.5 4.8 %add_convert_fusion.4 = bf16[384,2048]{1,0:T(8,128)(2,1)} fusion(f32[384,2048]{1,0:T(8,128)} %fusion.22, bf16[512,2048]{1,0:T(8,128)(2,1)} %param.13, bf16[384,512]{1,0:T(8,128)(2,1)} %reduce-scatter.4.cloned.1.call-done, f32[384]{0:T(512)S(1)} %convert_element_type.103), kind=kOutput, calls=%fused_computation.23 | convolution fusion | flops 807469056 | bytes 7210496 | tf_op jit(solution)/shard_map/dot_general | solution.py:62
  159.3 0.0 reduce-scatter.6.cloned.1.call-update
  159.3 0.3 reduce-scatter.8.cloned.1.call-start
  159.7 0.9 select_n.30
  160.6 2.5 slice_reduce_fusion.14
  163.1 23.5 %reduce-scatter.6.cloned.1.call-done = bf16[384,512]{1,0:T(8,128)(2,1)} async-done(((bf16[384,2048]{1,0:T(8,128)(2,1)}), bf16[384,512]{1,0:T(8,128)(2,1)}) %reduce-scatter.6.cloned.1.call-update) | async-done | bytes 393232 | tf_op jit(solution)/shard_map/reduce_scatter | solution.py:64
  186.6 1.0 broadcast_maximum_fusion
  187.7 4.7 %convolution_divide_fusion = f32[2048,256]{1,0:T(8,128)} fusion(s32[2048]{0:T(1024)S(1)} %get-tuple-element.16, s32[2048]{0:T(1024)S(1)} %get-tuple-element.17, s32[2048]{0:T(1024)S(1)} %get-tuple-element.18, s32[2048]{0:T(1024)S(1)} %get-tuple-element.19, s32[2048]{0:T(1024)S(1)} %get-tuple-element.15, bf16[512,256]{1,0:T(8,128)(2,1)S(1)} %copy-done.4, ...), kind=kOutput, calls=%fused_computation.30 | convolution fusion | flops 515932160 | bytes 2801664 | tf_op jit(solution)/shard_map/dot_general | solution.py:70
  192.4 1.9 fusion.17
  194.2 0.0 reduce-scatter.8.cloned.1.call-update
  194.2 138.1 %reduce-scatter.8.cloned.1.call-done = f32[64,256]{1,0:T(8,128)} async-done(((f32[2048,256]{1,0:T(8,128)}), f32[64,256]{1,0:T(8,128)}) %reduce-scatter.8.cloned.1.call-update) | async-done | bytes 65552 | tf_op jit(solution)/shard_map/reduce_scatter | solution.py:75
  332.4 0.9 multiply_reduce_fusion
  333.3 1.5 multiply_convert_fusion
  (21 shorter events, 0.2 us)
Async XLA Ops:
  6.5 73.2 %copy-start = (bf16[512,2048]{1,0:T(8,128)(2,1)S(1)}, bf16[512,2048]{1,0:T(8,128)(2,1)}, u32[]{:S(2)}) copy-start(bf16[512,2048]{1,0:T(8,128)(2,1)} %param.12) | copy-start | bytes 6291460
  6.5 148.0 %reduce-scatter.4.cloned.1.call-start = ((), (), s32[]{:S(2)}) async-start(), calls=%async_computation.3 | async-start | bytes 3538944 | tf_op jit(solution)/shard_map/reduce_scatter | solution.py:57
  51.7 7.9 %copy-start.2 = (bf16[1024,512]{1,0:T(8,128)(2,1)S(1)}, bf16[1024,512]{1,0:T(8,128)(2,1)}, u32[]{:S(2)}) copy-start(bf16[1024,512]{1,0:T(8,128)(2,1)} %param.10) | copy-start | bytes 3145732
  51.7 7.9 %copy-start.5 = (bf16[4,512]{1,0:T(4,128)(2,1)S(1)}, bf16[4,512]{1,0:T(4,128)(2,1)}, u32[]{:S(2)}) copy-start(bf16[4,512]{1,0:T(4,128)(2,1)} %param.11) | copy-start | bytes 12292
  79.1 0.7 copy-start.3
  79.1 107.5 %reduce-scatter.6.cloned.1.call-start = ((), (), s32[]{:S(2)}) async-start(), calls=%async_computation.4 | async-start | bytes 1966080 | tf_op jit(solution)/shard_map/reduce_scatter | solution.py:64
  159.3 173.0 %reduce-scatter.8.cloned.1.call-start = ((), (), s32[]{:S(2)}) async-start(), calls=%async_computation.5 | async-start | bytes 2162688 | tf_op jit(solution)/shard_map/reduce_scatter | solution.py:75
  160.6 27.1 %copy-start.4 = (bf16[512,256]{1,0:T(8,128)(2,1)S(1)}, bf16[512,256]{1,0:T(8,128)(2,1)}, u32[]{:S(2)}) copy-start(bf16[512,256]{1,0:T(8,128)(2,1)} %param.15) | copy-start | bytes 786436
  187.6 4.7 %copy-start.1 = (bf16[512,256]{1,0:T(8,128)(2,1)S(1)}, bf16[512,256]{1,0:T(8,128)(2,1)}, u32[]{:S(2)}) copy-start(bf16[512,256]{1,0:T(8,128)(2,1)} %param.14) | copy-start | bytes 786436
Sparse Core Ops, SparseCore 0:
  79.2 75.2 reduce-scatter.3
  159.5 27.0 reduce-scatter.5
  194.4 137.9 reduce-scatter.7
where the time goes:
time: 342 us; the launch traced here: 341 us
  waiting for transfers between devices  233 us (68%)
  matrix products  34.4 us (10%)
  blocking collectives  32.4 us (9%)
  local copies, waits for them, and re-layouts  20 us (6%)
  between operations  13.3 us (4%)
  other arithmetic  8.17 us (2%)
    reduce_scatter x1, waiting for transfers between devices, body(): lax.psum_scatter(mixed, ('node', 'feat'), scatter_dimension=0, tiled=True)  138 us
    reduce_scatter x1, waiting for transfers between devices, body(): lax.psum_scatter(sums.astype(jnp.bfloat16), 'node', scatter_dimension=0,...  71.1 us
    all_gather x1, blocking collectives, body(): everyone = lax.all_gather(packed, 'node', axis=0, tiled=True)  32.4 us
    reduce_scatter x1, waiting for transfers between devices, body(): lax.psum_scatter(part.astype(jnp.bfloat16), 'feat', scatter_dimension=1,...  23.5 us
    dot_general x1, matrix products, body(): sums = jnp.dot(matrix_one, combined, preferred_element_type=jnp.float32)  19.4 us
    slice x2, local copies, waits for them, and re-layouts, count_matrix(): total = total + (local[:, k:k + 1] == columns).astype(jnp.float32)  10.4 us
  transfers between devices with their start and end apart: 3, of which 3 were waited for; matrix products, arithmetic and copies ran while one was open for 2% of the time, Pallas kernels for 0%

commit v1 on v0

--- a/solution.py
+++ b/solution.py
@@ -2,6 +2,13 @@
 import jax.numpy as jnp
 from jax import lax
 from jax.sharding import PartitionSpec as P
+
+
+def read_array(ax_name, local_block):
+    side_arr = lax.axis_size(ax_name)
+    answer = jnp.concatenate(side_arr * [local_block], axis=0)
+    shaped = lax.all_to_all(answer, ax_name, 0, 0, tiled=True)
+    return shaped
 
 
 def count_matrix(local, width):
@@ -38,7 +45,7 @@
     packed = jnp.concatenate([lists_one.reshape(-1), lists_two.reshape(-1), second_counts]).reshape(
         1, -1
     )
-    everyone = lax.all_gather(packed, "node", axis=0, tiled=True)
+    everyone = read_array("node", packed)
     cut_one = front_here * fan_one
     cut_two = cut_one + targets_here * fan_two
     all_one = everyone[:, :cut_one].reshape(shards * front_here, fan_one)

time: 342 us -> 323 us (0.944)
  blocking collectives: 32.4 us -> 0 us
  starting transfers between devices: 0.31 us -> 7.62 us
  waiting for transfers between devices: 233 us -> 238 us
    all_gather x1 -> x0, blocking collectives: 32.4 us -> none  [body(): everyone = lax.all_gather(packed, 'node', axis=0, tiled=True)]
    all_to_all x0 -> x1, waiting for transfers between devices: none -> 7.57 us  [read_array(): shaped = lax.all_to_all(answer, ax_name, 0, 0, tiled=True)]
    all_to_all x0 -> x1, starting transfers between devices: none -> 7.28 us  [read_array(): shaped = lax.all_to_all(answer, ax_name, 0, 0, tiled=True)]
  transfers between devices with their start and end apart: 3 -> 4, of which waited for: 3 -> 4; matrix products, arithmetic and copies ran while one was open for 2% -> 2% of each run, Pallas kernels for 0% -> 0%
where the time goes in v1:
time: 323 us
  waiting for transfers between devices  238 us (74%)
  matrix products  34.4 us (11%)
  local copies, waits for them, and re-layouts  20.7 us (6%)
  between operations  13.3 us (4%)
  other arithmetic  8.17 us (3%)
  starting transfers between devices  7.62 us (2%)
    reduce_scatter x1, waiting for transfers between devices, body(): lax.psum_scatter(mixed, ('node', 'feat'), scatter_dimension=0, tiled=True)  139 us
    reduce_scatter x1, waiting for transfers between devices, body(): lax.psum_scatter(sums.astype(jnp.bfloat16), 'node', scatter_dimension=0,...  68.6 us
    reduce_scatter x1, waiting for transfers between devices, body(): lax.psum_scatter(part.astype(jnp.bfloat16), 'feat', scatter_dimension=1,...  23.5 us
    dot_general x1, matrix products, body(): sums = jnp.dot(matrix_one, combined, preferred_element_type=jnp.float32)  19.4 us
    slice x2, local copies, waits for them, and re-layouts, count_matrix(): total = total + (local[:, k:k + 1] == columns).astype(jnp.float32)  10.4 us
    all_to_all x1, waiting for transfers between devices, read_array(): shaped = lax.all_to_all(answer, ax_name, 0, 0, tiled=True)  7.57 us
    all_to_all x1, starting transfers between devices, read_array(): shaped = lax.all_to_all(answer, ax_name, 0, 0, tiled=True)  7.28 us
  transfers between devices with their start and end apart: 4, of which 4 were waited for; matrix products, arithmetic and copies ran while one was open for 2% of the time, Pallas kernels for 0%

profile of v1, /device:TPU:0, one launch (start us, length us, event | category | flops | bytes accessed | tf_op | source)
XLA Modules:
  0.0 322.6 jit_solution(143878566394149892)
XLA Ops:
  6.5 0.9 fusion.27
  7.4 0.1 copy.16
  7.5 0.2 reshape.59
  7.7 0.7 fusion.25
  8.5 0.1 copy.15
  8.6 0.1 reshape.58
  8.8 0.7 pad_add_fusion
  9.5 0.8 concatenate.10
  10.2 7.3 %all-to-all-start = ((s32[8,1,5376]{2,1,0:T(1,128)}), s32[8,1,5376]{2,1,0:T(1,128)S(1)}, u32[]{:S(2)}, u32[]{:S(2)}) async-start(s32[8,1,5376]{2,1,0:T(1,128)} %concatenate.10), calls=%async_computation | async-start | bytes 344064 | tf_op jit(solution)/shard_map/all_to_all | solution.py:10
  17.5 0.0 reduce-scatter.4.cloned.1.call-start
  17.6 7.6 %all-to-all-done = s32[8,1,5376]{2,1,0:T(1,128)S(1)} async-done(((s32[8,1,5376]{2,1,0:T(1,128)}), s32[8,1,5376]{2,1,0:T(1,128)S(1)}, u32[]{:S(2)}, u32[]{:S(2)}) %all-to-all-start) | async-done | bytes 172064 | tf_op jit(solution)/shard_map/all_to_all | solution.py:10
  25.2 1.8 ge.24
  27.0 2.8 reshape.61
  29.8 2.8 sub.31
  32.6 2.3 and_select_fusion
  34.9 7.9 %slice_reduce_fusion.9 = (s32[3072]{0:T(1024)S(1)}, s32[3072]{0:T(1024)S(1)}, s32[3072]{0:T(1024)S(1)}, s32[3072]{0:T(1024)S(1)}, s32[3072]{0:T(1024)S(1)}, /*in...) fusion(s32[3072,10]{1,0:T(8,128)S(1)} %and_select_fusion), kind=kLoop, calls=%fused_computation.40 | loop fusion | bytes 245760 | tf_op jit(solution)/shard_map/slice | solution.py:18
  42.9 19.4 %fusion.11 = bf16[3072,512]{1,0:T(8,128)(2,1)} fusion(s32[3072]{0:T(1024)S(1)} %get-tuple-element.6, s32[3072]{0:T(1024)S(1)} %get-tuple-element.7, s32[3072]{0:T(1024)S(1)} %get-tuple-element.8, s32[3072]{0:T(1024)S(1)} %get-tuple-element.9, s32[3072]{0:T(1024)S(1)} %get-tuple-element.10, s32[3072]{0:T(1024)S(1)} %get-tuple-element.11, ...), kind=kOutput, calls=%fused_computation.22 | convolution fusion | flops 3332227072 | bytes 4321280 | tf_op jit(solution)/shard_map/dot_general | solution.py:63
  62.3 0.0 reduce-scatter.6.cloned.1.call-start
  62.3 0.6 copy-done.3
  63.0 3.6 %fusion.22 = f32[384,2048]{1,0:T(8,128)} fusion(bf16[512,2048]{1,0:T(8,128)(2,1)S(1)} %copy-done, bf16[1024,512]{1,0:T(8,128)(2,1)} %param.10), kind=kOutput, calls=%fused_computation.60 | convolution fusion | flops 805306368 | bytes 5636096 | tf_op jit(solution)/shard_map/dot_general | solution.py:68
  66.6 68.6 %reduce-scatter.4.cloned.1.call-done = bf16[384,512]{1,0:T(8,128)(2,1)} async-done(((bf16[3072,512]{1,0:T(8,128)(2,1)}), bf16[384,512]{1,0:T(8,128)(2,1)}) %reduce-scatter.4.cloned.1.call-update) | async-done | bytes 393232 | tf_op jit(solution)/shard_map/reduce_scatter | solution.py:64
  135.2 4.8 %add_convert_fusion.4 = bf16[384,2048]{1,0:T(8,128)(2,1)} fusion(f32[384,2048]{1,0:T(8,128)} %fusion.22, bf16[512,2048]{1,0:T(8,128)(2,1)} %param.13, bf16[384,512]{1,0:T(8,128)(2,1)} %reduce-scatter.4.cloned.1.call-done, f32[384]{0:T(512)S(1)} %convert_element_type.103), kind=kOutput, calls=%fused_computation.23 | convolution fusion | flops 807469056 | bytes 7210496 | tf_op jit(solution)/shard_map/dot_general | solution.py:69
  140.1 0.3 reduce-scatter.8.cloned.1.call-start
  140.4 0.9 select_n.30
  141.3 2.5 slice_reduce_fusion.14
  143.8 23.5 %reduce-scatter.6.cloned.1.call-done = bf16[384,512]{1,0:T(8,128)(2,1)} async-done(((bf16[384,2048]{1,0:T(8,128)(2,1)}), bf16[384,512]{1,0:T(8,128)(2,1)}) %reduce-scatter.6.cloned.1.call-update) | async-done | bytes 393232 | tf_op jit(solution)/shard_map/reduce_scatter | solution.py:71
  167.3 1.0 broadcast_maximum_fusion
  168.3 4.7 %convolution_divide_fusion = f32[2048,256]{1,0:T(8,128)} fusion(s32[2048]{0:T(1024)S(1)} %get-tuple-element.16, s32[2048]{0:T(1024)S(1)} %get-tuple-element.17, s32[2048]{0:T(1024)S(1)} %get-tuple-element.18, s32[2048]{0:T(1024)S(1)} %get-tuple-element.19, s32[2048]{0:T(1024)S(1)} %get-tuple-element.15, bf16[512,256]{1,0:T(8,128)(2,1)S(1)} %copy-done.4, ...), kind=kOutput, calls=%fused_computation.30 | convolution fusion | flops 515932160 | bytes 2801664 | tf_op jit(solution)/shard_map/dot_general | solution.py:77
  173.0 1.9 fusion.17
  174.9 138.6 %reduce-scatter.8.cloned.1.call-done = f32[64,256]{1,0:T(8,128)} async-done(((f32[2048,256]{1,0:T(8,128)}), f32[64,256]{1,0:T(8,128)}) %reduce-scatter.8.cloned.1.call-update) | async-done | bytes 65552 | tf_op jit(solution)/shard_map/reduce_scatter | solution.py:82
  313.6 0.9 multiply_reduce_fusion
  314.5 1.5 multiply_convert_fusion
  (22 shorter events, 0.2 us)
Async XLA Ops:
  6.5 56.4 %copy-start = (bf16[512,2048]{1,0:T(8,128)(2,1)S(1)}, bf16[512,2048]{1,0:T(8,128)(2,1)}, u32[]{:S(2)}) copy-start(bf16[512,2048]{1,0:T(8,128)(2,1)} %param.12) | copy-start | bytes 6291460
  10.2 14.9 %all-to-all-start = ((s32[8,1,5376]{2,1,0:T(1,128)}), s32[8,1,5376]{2,1,0:T(1,128)S(1)}, u32[]{:S(2)}, u32[]{:S(2)}) async-start(s32[8,1,5376]{2,1,0:T(1,128)} %concatenate.10), calls=%async_computation | async-start | bytes 344064 | tf_op jit(solution)/shard_map/all_to_all | solution.py:10
  17.5 117.7 %reduce-scatter.4.cloned.1.call-start = ((), (), s32[]{:S(2)}) async-start(), calls=%async_computation.4 | async-start | bytes 3538944 | tf_op jit(solution)/shard_map/reduce_scatter | solution.py:64
  34.9 7.9 %copy-start.2 = (bf16[1024,512]{1,0:T(8,128)(2,1)S(1)}, bf16[1024,512]{1,0:T(8,128)(2,1)}, u32[]{:S(2)}) copy-start(bf16[1024,512]{1,0:T(8,128)(2,1)} %param.10) | copy-start | bytes 3145732
  34.9 7.9 %copy-start.5 = (bf16[4,512]{1,0:T(4,128)(2,1)S(1)}, bf16[4,512]{1,0:T(4,128)(2,1)}, u32[]{:S(2)}) copy-start(bf16[4,512]{1,0:T(4,128)(2,1)} %param.11) | copy-start | bytes 12292
  62.3 0.7 copy-start.3
  62.3 105.0 %reduce-scatter.6.cloned.1.call-start = ((), (), s32[]{:S(2)}) async-start(), calls=%async_computation.5 | async-start | bytes 1966080 | tf_op jit(solution)/shard_map/reduce_scatter | solution.py:71
  140.1 173.5 %reduce-scatter.8.cloned.1.call-start = ((), (), s32[]{:S(2)}) async-start(), calls=%async_computation.6 | async-start | bytes 2162688 | tf_op jit(solution)/shard_map/reduce_scatter | solution.py:82
  141.3 27.0 %copy-start.4 = (bf16[512,256]{1,0:T(8,128)(2,1)S(1)}, bf16[512,256]{1,0:T(8,128)(2,1)}, u32[]{:S(2)}) copy-start(bf16[512,256]{1,0:T(8,128)(2,1)} %param.15) | copy-start | bytes 786436
  168.3 4.7 %copy-start.1 = (bf16[512,256]{1,0:T(8,128)(2,1)S(1)}, bf16[512,256]{1,0:T(8,128)(2,1)}, u32[]{:S(2)}) copy-start(bf16[512,256]{1,0:T(8,128)(2,1)} %param.14) | copy-start | bytes 786436
Sparse Core Ops, SparseCore 0:
  62.4 72.7 reduce-scatter.3
  140.2 27.0 reduce-scatter.5
  175.1 138.4 reduce-scatter.7
